TPU v7x, 32 devices: a whole 2x2x4 slice. The times are simulated.
32 devices in a mesh: seq: 4 (over x, core), fsdp: 8 (over z, y).
Axes of the slice: x: 2, y: 2, z: 4, core: 2. Of those that a mesh axis runs over, the one named last changes fastest.
Arguments:
- layer_input: bfloat16 [8, 1536, 1024], P('fsdp', 'seq'), may hold values from -12 to 12
- query_weight: bfloat16 [1024, 1024], P('fsdp'), may hold values from -0.1875 to 0.1875
- key_weight: bfloat16 [1024, 1024], P('fsdp'), may hold values from -0.1875 to 0.1875
- value_weight: bfloat16 [1024, 1024], P('fsdp'), may hold values from -0.1875 to 0.1875
- output_weight: bfloat16 [1024, 1024], P('fsdp'), may hold values from -0.75 to 0.75
- query_bias: bfloat16 [1024], P('fsdp'), may hold values from -4 to 4
- value_bias: bfloat16 [1024], P('fsdp'), may hold values from -1.5 to 1.5
- output_bias: bfloat16 [1024], P('fsdp'), may hold values from -4 to 4
- attn_gain: bfloat16 [1024], P('fsdp'), may hold values from 0.5 to 1.5
- attn_shift: bfloat16 [1024], P('fsdp'), may hold values from -4 to 4
- in_weight: bfloat16 [1024, 4096], P('fsdp'), may hold values from -0.1875 to 0.1875
- in_bias: bfloat16 [4096], P('fsdp'), may hold values from -4 to 4
- out_weight: bfloat16 [4096, 1024], P('fsdp'), may hold values from -0.09375 to 0.09375
- out_bias: bfloat16 [1024], P('fsdp'), may hold values from -4 to 4
- out_gain: bfloat16 [1024], P('fsdp'), may hold values from 0.5 to 1.5
- out_shift: bfloat16 [1024], P('fsdp'), may hold values from -4 to 4
- out_cotangent: bfloat16 [8, 1536, 1024], P('fsdp', 'seq'), may hold values from -6 to 6
Outputs:
- layer_output: bfloat16 [8, 1536, 1024], P('fsdp', 'seq')
- input_grad: float32 [8, 1536, 1024], P('fsdp', 'seq')
- query_weight_grad: float32 [1024, 1024], P('fsdp')
- key_weight_grad: float32 [1024, 1024], P('fsdp')
- value_weight_grad: float32 [1024, 1024], P('fsdp')
- output_weight_grad: float32 [1024, 1024], P('fsdp')
- query_bias_grad: float32 [1024], P('fsdp')
- value_bias_grad: float32 [1024], P('fsdp')
- output_bias_grad: float32 [1024], P('fsdp')
- attn_gain_grad: float32 [1024], P('fsdp')
- attn_shift_grad: float32 [1024], P('fsdp')
- in_weight_grad: float32 [1024, 4096], P('fsdp')
- in_bias_grad: float32 [4096], P('fsdp')
- out_weight_grad: float32 [4096, 1024], P('fsdp')
- out_bias_grad: float32 [1024], P('fsdp')
- out_gain_grad: float32 [1024], P('fsdp')
- out_shift_grad: float32 [1024], P('fsdp')
- rms_values: float32 [5], replicated
All inputs are finite; a program needn't handle non-finite values.
Results may differ from a plain program's by a relative error of at most 0.015.
Values may be sent and summed in bfloat16 or wider, within the bound.
A program may use at most 192 MiB of HBM per device.

v0:
```python
import jax
import jax.numpy as jnp
from jax import lax
from jax.sharding import PartitionSpec as P

HD = 64


def layer_norm(stream, gain, shift):
    centre = stream - jnp.mean(stream, axis=-1, keepdims=True)
    variance = jnp.mean(centre * centre, axis=-1, keepdims=True)
    return centre * lax.rsqrt(variance + 1e-05) * gain + shift


def gelu_exact(inputs):
    return jax.nn.gelu(inputs, approximate=False)


def column_sums(matrix):
    return jnp.sum(matrix.astype(jnp.float32), axis=0)


def local(
    layer_input,
    query_weight,
    key_weight,
    value_weight,
    output_weight,
    query_bias,
    value_bias,
    output_bias,
    attn_gain,
    attn_shift,
    in_weight,
    in_bias,
    out_weight,
    out_bias,
    out_gain,
    out_shift,
    out_cotangent,
):
    half = jnp.bfloat16
    single = jnp.float32
    fsdp_count = lax.axis_size("fsdp")
    seq_count = lax.axis_size("seq")
    (
        full_query,
        full_key,
        full_value,
        full_output,
        bias_query,
        bias_value,
        bias_output,
        gain_one,
        shift_one,
    ) = (
        lax.all_gather(query_weight, "fsdp", axis=0, tiled=True),
        lax.all_gather(key_weight, "fsdp", axis=0, tiled=True),
        lax.all_gather(value_weight, "fsdp", axis=0, tiled=True),
        lax.all_gather(output_weight, "fsdp", axis=0, tiled=True),
        lax.all_gather(query_bias, "fsdp", axis=0, tiled=True),
        lax.all_gather(value_bias, "fsdp", axis=0, tiled=True),
        lax.all_gather(output_bias, "fsdp", axis=0, tiled=True),
        lax.all_gather(attn_gain, "fsdp", axis=0, tiled=True),
        lax.all_gather(attn_shift, "fsdp", axis=0, tiled=True),
    )
    full_in, full_out, bias_in, bias_out, gain_two, shift_two = (
        lax.all_gather(in_weight, "fsdp", axis=0, tiled=True),
        lax.all_gather(out_weight, "fsdp", axis=0, tiled=True),
        lax.all_gather(in_bias, "fsdp", axis=0, tiled=True),
        lax.all_gather(out_bias, "fsdp", axis=0, tiled=True),
        lax.all_gather(out_gain, "fsdp", axis=0, tiled=True),
        lax.all_gather(out_shift, "fsdp", axis=0, tiled=True),
    )
    model_width = layer_input.shape[-1]
    tokens = layer_input.reshape(-1, model_width)
    token_rows = tokens.shape[0]
    tokens_single = tokens.astype(single)
    query_rows = (
        jnp.dot(tokens, full_query, preferred_element_type=single) + bias_query.astype(single)
    ).astype(half)
    key_rows = jnp.dot(tokens, full_key, preferred_element_type=single).astype(half)
    value_rows = (
        jnp.dot(tokens, full_value, preferred_element_type=single) + bias_value.astype(single)
    ).astype(half)
    stacked = jnp.stack([query_rows, key_rows, value_rows])
    regrouped = lax.all_to_all(stacked, "seq", split_axis=2, concat_axis=1, tiled=True)
    seq_length = regrouped.shape[1]
    local_width = regrouped.shape[2]
    heads_here = local_width // HD
    query_heads = regrouped[0].reshape(seq_length, heads_here, HD)
    key_heads = regrouped[1].reshape(seq_length, heads_here, HD)
    value_heads = regrouped[2].reshape(seq_length, heads_here, HD)
    block_rows = min(512, seq_length)
    block_count = seq_length // block_rows
    query_blocks = query_heads.reshape(block_count, block_rows, heads_here, HD)

    def forward_block(query_block):
        scores = (
            jnp.einsum("qhd,khd->hqk", query_block, key_heads, preferred_element_type=single)
            * 0.125
        )
        row_max = jnp.max(scores, axis=-1, keepdims=True)
        exp_scores = jnp.exp(scores - row_max)
        row_total = jnp.sum(exp_scores, axis=-1, keepdims=True)
        attn_probs = exp_scores / row_total
        block_out = jnp.einsum(
            "hqk,khd->qhd", attn_probs.astype(half), value_heads, preferred_element_type=single
        )
        return (block_out.astype(half), row_max[..., 0] + jnp.log(row_total[..., 0]))

    mixed_blocks, log_total = lax.map(forward_block, query_blocks)
    attn_mixed = mixed_blocks.reshape(seq_length, local_width)
    regathered = lax.all_to_all(attn_mixed, "seq", split_axis=0, concat_axis=1, tiled=True)
    attn_out = jnp.dot(regathered, full_output, preferred_element_type=single) + bias_output.astype(
        single
    )
    normed, pull_first = jax.vjp(
        layer_norm, tokens_single + attn_out, gain_one.astype(single), shift_one.astype(single)
    )
    normed_low = normed.astype(half)
    hidden_pre = jnp.dot(normed_low, full_in, preferred_element_type=single) + bias_in.astype(
        single
    )
    hidden_single, pull_gelu = jax.vjp(gelu_exact, hidden_pre)
    hidden = hidden_single.astype(half)
    branch = jnp.dot(hidden, full_out, preferred_element_type=single) + bias_out.astype(single)
    layer_out, pull_second = jax.vjp(
        layer_norm, normed + branch, gain_two.astype(single), shift_two.astype(single)
    )
    squares = jnp.stack(
        [
            jnp.sum(tokens_single * tokens_single),
            jnp.sum(attn_out * attn_out),
            jnp.sum(normed * normed),
            jnp.sum(branch * branch),
            jnp.sum(layer_out * layer_out),
        ]
    )
    square_sums = lax.psum(squares, ("seq", "fsdp"))
    rms_values = jnp.sqrt(square_sums / single(token_rows * model_width * seq_count * fsdp_count))
    cotangent = out_cotangent.reshape(token_rows, model_width).astype(single)
    grad_stream, grad_gain_two, grad_shift_two = pull_second(cotangent)
    grad_branch = grad_stream.astype(half)
    grad_bias_out = column_sums(grad_branch)
    grad_out = jnp.dot(hidden.T, grad_branch, preferred_element_type=single)
    grad_hidden = jnp.dot(grad_branch, full_out.T, preferred_element_type=single)
    grad_pre = pull_gelu(grad_hidden)[0].astype(half)
    grad_bias_in = column_sums(grad_pre)
    grad_in = jnp.dot(normed_low.T, grad_pre, preferred_element_type=single)
    grad_normed = grad_stream + jnp.dot(grad_pre, full_in.T, preferred_element_type=single)
    grad_h, grad_gain_one, grad_shift_one = pull_first(grad_normed)
    mlp_summed = (
        lax.psum_scatter(grad_in, "fsdp", scatter_dimension=0, tiled=True),
        lax.psum_scatter(grad_out, "fsdp", scatter_dimension=0, tiled=True),
        lax.psum_scatter(grad_bias_in, "fsdp", scatter_dimension=0, tiled=True),
        lax.psum_scatter(grad_bias_out, "fsdp", scatter_dimension=0, tiled=True),
        lax.psum_scatter(grad_gain_two, "fsdp", scatter_dimension=0, tiled=True),
        lax.psum_scatter(grad_shift_two, "fsdp", scatter_dimension=0, tiled=True),
    )
    grad_attn = grad_h.astype(half)
    grad_bias_output = column_sums(grad_attn)
    grad_output = jnp.dot(regathered.T, grad_attn, preferred_element_type=single)
    grad_regathered = jnp.dot(grad_attn, full_output.T, preferred_element_type=single).astype(half)
    grad_mixed = lax.all_to_all(grad_regathered, "seq", split_axis=1, concat_axis=0, tiled=True)
    grad_mixed_blocks = grad_mixed.reshape(block_count, block_rows, heads_here, HD)

    def backward_block(grad_carry, block_parts):
        grad_keys, grad_values = grad_carry
        query_block, block_total, grad_block = block_parts
        scores = (
            jnp.einsum("qhd,khd->hqk", query_block, key_heads, preferred_element_type=single)
            * 0.125
        )
        attn_probs = jnp.exp(scores - block_total[..., None])
        grad_probs = jnp.einsum(
            "qhd,khd->hqk", grad_block, value_heads, preferred_element_type=single
        )
        row_delta = jnp.sum(attn_probs * grad_probs, axis=-1, keepdims=True)
        grad_scores = (attn_probs * (grad_probs - row_delta)).astype(half)
        grad_query = (
            jnp.einsum("hqk,khd->qhd", grad_scores, key_heads, preferred_element_type=single)
            * 0.125
        )
        grad_keys = (
            grad_keys
            + jnp.einsum("hqk,qhd->khd", grad_scores, query_block, preferred_element_type=single)
            * 0.125
        )
        grad_values = grad_values + jnp.einsum(
            "hqk,qhd->khd", attn_probs.astype(half), grad_block, preferred_element_type=single
        )
        return ((grad_keys, grad_values), grad_query.astype(half))

    zero_grads = jnp.zeros((seq_length, heads_here, HD), single)
    (grad_keys, grad_values), grad_query_blocks = lax.scan(
        backward_block, (zero_grads, zero_grads), (query_blocks, log_total, grad_mixed_blocks)
    )
    grad_heads = jnp.stack(
        [
            grad_query_blocks.reshape(seq_length, local_width),
            grad_keys.reshape(seq_length, local_width).astype(half),
            grad_values.reshape(seq_length, local_width).astype(half),
        ]
    )
    grad_tokens = lax.all_to_all(grad_heads, "seq", split_axis=1, concat_axis=2, tiled=True)
    grad_query_rows = grad_tokens[0]
    grad_key_rows = grad_tokens[1]
    grad_value_rows = grad_tokens[2]
    grad_query = jnp.dot(tokens.T, grad_query_rows, preferred_element_type=single)
    grad_key = jnp.dot(tokens.T, grad_key_rows, preferred_element_type=single)
    grad_value = jnp.dot(tokens.T, grad_value_rows, preferred_element_type=single)
    grad_bias_query = column_sums(grad_query_rows)
    grad_bias_value = column_sums(grad_value_rows)
    input_grad = grad_h + jnp.dot(grad_query_rows, full_query.T, preferred_element_type=single)
    input_grad = input_grad + jnp.dot(grad_key_rows, full_key.T, preferred_element_type=single)
    input_grad = input_grad + jnp.dot(grad_value_rows, full_value.T, preferred_element_type=single)
    attn_summed = (
        lax.psum_scatter(grad_query, "fsdp", scatter_dimension=0, tiled=True),
        lax.psum_scatter(grad_key, "fsdp", scatter_dimension=0, tiled=True),
        lax.psum_scatter(grad_value, "fsdp", scatter_dimension=0, tiled=True),
        lax.psum_scatter(grad_output, "fsdp", scatter_dimension=0, tiled=True),
        lax.psum_scatter(grad_bias_query, "fsdp", scatter_dimension=0, tiled=True),
        lax.psum_scatter(grad_bias_value, "fsdp", scatter_dimension=0, tiled=True),
        lax.psum_scatter(grad_bias_output, "fsdp", scatter_dimension=0, tiled=True),
        lax.psum_scatter(grad_gain_one, "fsdp", scatter_dimension=0, tiled=True),
        lax.psum_scatter(grad_shift_one, "fsdp", scatter_dimension=0, tiled=True),
    )
    summed = lax.psum(
        (
            attn_summed[0],
            attn_summed[1],
            attn_summed[2],
            attn_summed[3],
            attn_summed[4],
            attn_summed[5],
            attn_summed[6],
            attn_summed[7],
            attn_summed[8],
            mlp_summed[0],
            mlp_summed[1],
            mlp_summed[2],
            mlp_summed[3],
            mlp_summed[4],
            mlp_summed[5],
        ),
        "seq",
    )
    results = (
        summed[0],
        summed[1],
        summed[2],
        summed[3],
        summed[4],
        summed[5],
        summed[6],
        summed[7],
        summed[8],
        summed[9],
        summed[11],
        summed[10],
        summed[12],
        summed[13],
        summed[14],
    )
    return (
        layer_out.astype(half).reshape(layer_input.shape),
        input_grad.reshape(layer_input.shape),
        results[0],
        results[1],
        results[2],
        results[3],
        results[4],
        results[5],
        results[6],
        results[7],
        results[8],
        results[9],
        results[10],
        results[11],
        results[12],
        results[13],
        results[14],
        rms_values,
    )


def solution(mesh):
    placed = (
        P("fsdp", "seq", None),
        P("fsdp", None),
        P("fsdp", None),
        P("fsdp", None),
        P("fsdp", None),
        P("fsdp"),
        P("fsdp"),
        P("fsdp"),
        P("fsdp"),
        P("fsdp"),
        P("fsdp", None),
        P("fsdp"),
        P("fsdp", None),
        P("fsdp"),
        P("fsdp"),
        P("fsdp"),
        P("fsdp", "seq", None),
    )
    return jax.shard_map(
        local,
        mesh=mesh,
        in_specs=placed,
        out_specs=(
            P("fsdp", "seq", None),
            P("fsdp", "seq", None),
            P("fsdp", None),
            P("fsdp", None),
            P("fsdp", None),
            P("fsdp", None),
            P("fsdp"),
            P("fsdp"),
            P("fsdp"),
            P("fsdp"),
            P("fsdp"),
            P("fsdp", None),
            P("fsdp"),
            P("fsdp", None),
            P("fsdp"),
            P("fsdp"),
            P("fsdp"),
            P(),
        ),
        check_vma=False,
    )
```

profile of v0, /device:TPU:0, one launch (start us, length us, event | category | flops | bytes accessed | tf_op | source)
XLA Modules:
  0.0 1655.2 jit_solution(8044954652545755404)
XLA Ops:
  10.6 22.4 %all-gather = bf16[8,1,128]{2,1,0:T(2,128)(2,1)S(1)} all-gather(bf16[1,1,128]{2,1,0:T(2,128)(2,1)} %bitcast.251), channel_id=1, replica_groups=mesh['seq'=4,'fsdp'=8] {'fsdp'}, dimensions={0}, use_global_device_ids=true | all-gather | bytes 2304 | tf_op jit(solution)/shard_map/all_gather | solution.py:61
  32.9 16.5 all-gather.1
  49.5 12.7 all-gather.18.cloned.1.call-done
  65.0 47.1 %all-gather.16.cloned.1.call-done = bf16[1024,1024]{1,0:T(8,128)(2,1)} async-done(((bf16[128,1024]{1,0:T(8,128)(2,1)}), bf16[1024,1024]{1,0:T(8,128)(2,1)}) %all-gather.16.cloned.1.call-update) | async-done | bytes 2097168 | tf_op jit(solution)/shard_map/all_gather | solution.py:57
  112.1 3.5 fusion.54
  115.6 46.5 %all-gather.20.cloned.1.call-done = bf16[1024,1024]{1,0:T(8,128)(2,1)} async-done(((bf16[128,1024]{1,0:T(8,128)(2,1)}), bf16[1024,1024]{1,0:T(8,128)(2,1)}) %all-gather.20.cloned.1.call-update) | async-done | bytes 2097168 | tf_op jit(solution)/shard_map/all_gather | solution.py:59
  165.0 3.8 copy.66
  168.8 3.8 all-to-all-start
  173.1 36.3 %all-to-all-done = bf16[3,384,1024]{1,0,2:T(4,128)(2,1)S(1)} async-done(((bf16[3,384,1024]{1,0,2:T(4,128)(2,1)}), bf16[3,384,1024]{1,0,2:T(4,128)(2,1)S(1)}, u32[]{:S(2)}, u32[]{:S(2)}) %all-to-all-start) | async-done | bytes 2359328 | tf_op jit(solution)/shard_map/all_to_all | solution.py:87
  218.6 25.2 %while.27 = (s32[]{:T(128)}, bf16[3,512,4,64]{1,3,2,0:T(8,128)(2,1)}, f32[3,4,512]{2,1,0:T(4,128)S(1)}, bf16[3,512,4,64]{1,3,2,0:T(8,128)(2,1)S(1)}, bf16[1536,4...) while((s32[]{:T(128)}, bf16[3,512,4,64]{1,3,2,0:T(8,128)(2,1)}, ...), condition=%wide.region_3.4_spmd, body=%wide.region_0.3_spmd.sunk | while | flops 833746944 | bytes 39912020 | solution.py:112
  222.8 4.2 fusion.137
  231.2 4.2 fusion.137
  239.6 4.2 fusion.137
  246.7 3.4 all_to_all.51
  252.2 4.2 all-to-all-start.1
  256.5 18.1 %all-gather.2 = bf16[8,1,128]{2,1,0:T(2,128)(2,1)S(1)} all-gather(bf16[1,1,128]{2,1,0:T(2,128)(2,1)S(1)} %bitcast.253), channel_id=1, replica_groups=mesh['seq'=4,'fsdp'=8] {'fsdp'}, dimensions={0}, use_global_device_ids=true | all-gather | bytes 2304 | tf_op jit(solution)/shard_map/all_gather | solution.py:63
  274.6 16.7 %all-gather.3 = bf16[8,1,128]{2,1,0:T(2,128)(2,1)S(1)} all-gather(bf16[1,1,128]{2,1,0:T(2,128)(2,1)S(1)} %bitcast.254), channel_id=1, replica_groups=mesh['seq'=4,'fsdp'=8] {'fsdp'}, dimensions={0}, use_global_device_ids=true | all-gather | bytes 2304 | tf_op jit(solution)/shard_map/all_gather | solution.py:64
  291.3 18.1 %all-gather.4 = bf16[8,1,128]{2,1,0:T(2,128)(2,1)S(1)} all-gather(bf16[1,1,128]{2,1,0:T(2,128)(2,1)S(1)} %bitcast.255), channel_id=1, replica_groups=mesh['seq'=4,'fsdp'=8] {'fsdp'}, dimensions={0}, use_global_device_ids=true | all-gather | bytes 2304 | tf_op jit(solution)/shard_map/all_gather | solution.py:65
  309.4 26.3 %all-gather.5 = bf16[8,1,512]{2,1,0:T(2,128)(2,1)S(1)} all-gather(bf16[1,1,512]{2,1,0:T(2,128)(2,1)S(1)} %reshape.201), channel_id=1, replica_groups=mesh['seq'=4,'fsdp'=8] {'fsdp'}, dimensions={0}, use_global_device_ids=true | all-gather | bytes 9216 | tf_op jit(solution)/shard_map/all_gather | solution.py:70
  335.7 16.3 all-gather.6
  352.0 18.5 %all-gather.7 = bf16[8,1,128]{2,1,0:T(2,128)(2,1)S(1)} all-gather(bf16[1,1,128]{2,1,0:T(2,128)(2,1)S(1)} %bitcast.257), channel_id=1, replica_groups=mesh['seq'=4,'fsdp'=8] {'fsdp'}, dimensions={0}, use_global_device_ids=true | all-gather | bytes 2304 | tf_op jit(solution)/shard_map/all_gather | solution.py:72
  370.5 16.3 all-gather.8
  386.9 3.9 fusion.75
  392.2 21.0 %multiply_convert_fusion.1 = (bf16[384,4096]{1,0:T(8,128)(2,1)}, f32[384,4096]{1,0:T(8,128)}, f32[384,4096]{1,0:T(8,128)}) fusion(f32[4096]{0:T(1024)S(1)} %bitcast.246, bf16[1024,4096]{1,0:T(8,128)(2,1)} %all-gather.24.cloned.1.call-done, f32[384,1024]{1,0:T(8,128)} %copy-done.7, f32[1024]{0:T(1024)S(1)} %bitcast.235, f32[1024]{0:T(1024)S(1)} %bitcast.230, ...), kind=kOutput, calls=%fused_computation.50 | convolution fusion | flops 3327000576 | bytes 25717760 | tf_op jit(solution)/shard_map/dot_general | solution.py:122
  413.2 49.8 %all-gather.26.cloned.1.call-done = bf16[4096,1024]{1,0:T(8,128)(2,1)} async-done(((bf16[512,1024]{1,0:T(8,128)(2,1)}), bf16[4096,1024]{1,0:T(8,128)(2,1)}) %all-gather.26.cloned.1.call-update) | async-done | bytes 8388624 | tf_op jit(solution)/shard_map/all_gather | solution.py:69
  463.0 9.0 fusion.73
  476.0 14.0 convert_reduce_fusion
  490.0 4.5 multiply_reduce_fusion.6
  502.2 4.2 all-to-all-start.2
  506.5 4.7 fusion.80
  511.3 6.9 all-to-all-done.2
  520.8 3.8 reshape.189
  527.8 84.8 %while.28 = (s32[]{:T(128)}, f32[1536,4,64]{0,2,1:T(8,128)}, f32[1536,4,64]{0,2,1:T(8,128)}, bf16[3,512,4,64]{1,3,2,0:T(8,128)(2,1)}, bf16[3,512,4,64]{1,3,2,0:T...) while((s32[]{:T(128)}, f32[1536,4,64]{0,2,1:T(8,128)}, ...), condition=%wide.region_14.15_spmd.clone, body=%wide.region_12.14_spmd.clone.sunk | while | flops 2053240832 | bytes 211347216 | solution.py:196
  529.7 4.9 multiply_reduce_fusion.13
  534.6 4.6 multiply_convert_fusion.3
  539.2 5.3 fusion.148
  544.5 6.4 fusion.150
  550.9 4.6 fusion.149
  557.4 4.9 multiply_reduce_fusion.13
  562.3 4.6 multiply_convert_fusion.3
  566.9 5.8 fusion.148
  572.7 6.3 fusion.150
  578.9 5.2 fusion.149
  586.0 4.9 multiply_reduce_fusion.13
  590.9 4.6 multiply_convert_fusion.3
  595.5 5.8 fusion.148
  601.2 6.2 fusion.150
  607.4 5.2 fusion.149
  618.9 4.3 copy.76
  623.2 39.6 %all_to_all.65 = bf16[3,1536,256]{2,0,1:T(4,128)(2,1)S(1)} all-to-all(bf16[3,1536,256]{2,0,1:T(4,128)(2,1)S(1)} %copy.76), channel_id=1, replica_groups=mesh['seq'=4,'fsdp'=8] {'seq'}, dimensions={1} | all-to-all | bytes 4718592 | tf_op jit(solution)/shard_map/all_to_all | solution.py:206
  666.1 4.3 convolution_bitcast_fusion
  672.9 4.6 convolution_bitcast_fusion.2
  679.8 4.5 convolution_bitcast_fusion.1
  685.0 13.1 fusion.68
  698.4 12.5 fusion.81
  711.0 45.6 %reduce-scatter.11.cloned.1.call-done = f32[128,1024]{0,1:T(8,128)} async-done(((f32[1024,1024]{0,1:T(8,128)}), f32[128,1024]{0,1:T(8,128)}) %reduce-scatter.11.cloned.1.call-update) | async-done | bytes 524304 | tf_op jit(solution)/shard_map/reduce_scatter | solution.py:221
  756.6 91.9 %reduce-scatter.7.cloned.1.call-done = f32[128,1024]{0,1:T(8,128)} async-done(((f32[1024,1024]{0,1:T(8,128)}), f32[128,1024]{0,1:T(8,128)}) %reduce-scatter.7.cloned.1.call-update) | async-done | bytes 524304 | tf_op jit(solution)/shard_map/reduce_scatter | solution.py:219
  848.5 92.2 %reduce-scatter.9.cloned.1.call-done = f32[128,1024]{0,1:T(8,128)} async-done(((f32[1024,1024]{0,1:T(8,128)}), f32[128,1024]{0,1:T(8,128)}) %reduce-scatter.9.cloned.1.call-update) | async-done | bytes 524304 | tf_op jit(solution)/shard_map/reduce_scatter | solution.py:220
  940.7 286.3 %reduce-scatter.15.cloned.1.call-done = f32[128,4096]{1,0:T(8,128)} async-done(((f32[1024,4096]{1,0:T(8,128)}), f32[128,4096]{1,0:T(8,128)}) %reduce-scatter.15.cloned.1.call-update) | async-done | bytes 2097168 | tf_op jit(solution)/shard_map/reduce_scatter | solution.py:154
  1227.0 285.9 %reduce-scatter.17.cloned.1.call-done = f32[512,1024]{1,0:T(8,128)} async-done(((f32[4096,1024]{1,0:T(8,128)}), f32[512,1024]{1,0:T(8,128)}) %reduce-scatter.17.cloned.1.call-update) | async-done | bytes 2097168 | tf_op jit(solution)/shard_map/reduce_scatter | solution.py:155
  1520.0 39.8 %psum.127 = f32[5]{0:T(128)S(1)} all-reduce(f32[5]{0:T(128)S(1)} %stack.45), channel_id=1, replica_groups=mesh['seq'=4,'fsdp'=8] {'seq','fsdp'}, use_global_device_ids=true, to_apply=%region_59.60 | all-reduce | flops 5 | bytes 40 | tf_op jit(solution)/shard_map/psum | solution.py:140
  1560.7 37.3 %all-reduce.9 = (f32[1024]{0:T(1024)S(1)}, f32[1024]{0:T(1024)S(1)}, f32[1024]{0:T(1024)S(1)}, f32[1024]{0:T(1024)S(1)}, f32[1024]{0:T(1024)S(1)}, /*index=5*/f3...) all-reduce(f32[1024]{0:T(1024)S(1)} %bitcast.244, ...), channel_id=6, replica_groups=mesh['seq'=4,'fsdp'=8] {'fsdp'}, use_global_device_ids=true, to_apply=%region_24.25.clone | all-reduce | flops 12288 | bytes 98304
  1598.7 7.0 all-reduce.10
  1613.2 23.7 %all-reduce.14.cloned.1.call-done = (f32[128,1024]{0,1:T(8,128)}, f32[128,1024]{0,1:T(8,128)}, f32[128,1024]{0,1:T(8,128)}, f32[128,1024]{1,0:T(8,128)}, f32[128,4096]{1,0:T(8,128)}, /*index=5*/f32[512,1024]{1,0:T(8,128)}) async-done(((f32[128,1024]{0,1:T(8,128)}, f32[128,1024]{0,1:T(8,128)}, f32[128,1024]{0,1:T(8,128)}, f32[128,1024]{1,0:T(8,128)}, f32[128,4096]{1,0:T(8,128)}, ...) | async-done | bytes 6291472 | tf_op jit(solution)/shard_map/psum | solution.py:229
  (236 shorter events, 102.6 us)
Async XLA Ops:
  7.2 55.0 %all-gather.18.cloned.1.call-start = ((), (), s32[]{:S(2)}) async-start(), calls=%async_computation.11 | async-start | bytes 2359296 | tf_op jit(solution)/shard_map/all_gather | solution.py:58
  7.9 104.2 %all-gather.16.cloned.1.call-start = ((), (), s32[]{:S(2)}) async-start(), calls=%async_computation.10 | async-start | bytes 2359296 | tf_op jit(solution)/shard_map/all_gather | solution.py:57
  8.7 153.4 %all-gather.20.cloned.1.call-start = ((), (), s32[]{:S(2)}) async-start(), calls=%async_computation.12 | async-start | bytes 2359296 | tf_op jit(solution)/shard_map/all_gather | solution.py:59
  9.4 377.5 %all-gather.22.cloned.1.call-start = ((), (), s32[]{:S(2)}) async-start(), calls=%async_computation.13 | async-start | bytes 2359296 | tf_op jit(solution)/shard_map/all_gather | solution.py:60
  10.0 102.1 %copy-start.10 = (bf16[1,384,1024]{2,1,0:T(8,128)(2,1)S(1)}, bf16[1,384,1024]{2,1,0:T(8,128)(2,1)}, u32[]{:S(2)}) copy-start(bf16[1,384,1024]{2,1,0:T(8,128)(2,1)} %param.21) | copy-start | bytes 2359300
  10.0 382.2 %all-gather.24.cloned.1.call-start = ((), (), s32[]{:S(2)}) async-start(), calls=%async_computation.14 | async-start | bytes 9437184 | tf_op jit(solution)/shard_map/all_gather | solution.py:68
  162.1 2.7 copy-start.17
  168.8 40.7 %all-to-all-start = ((bf16[3,384,1024]{1,0,2:T(4,128)(2,1)}), bf16[3,384,1024]{1,0,2:T(4,128)(2,1)S(1)}, u32[]{:S(2)}, u32[]{:S(2)}) async-start(bf16[3,384,1024]{1,0,2:T(4,128)(2,1)} %copy.66), calls=%async_computation | async-start | bytes 6291456 | tf_op jit(solution)/shard_map/all_to_all | solution.py:87
  172.5 290.4 %all-gather.26.cloned.1.call-start = ((), (), s32[]{:S(2)}) async-start(), calls=%async_computation.15 | async-start | bytes 9437184 | tf_op jit(solution)/shard_map/all_gather | solution.py:69
  243.8 12.6 copy-start.36
  243.8 30.7 %copy-start.37 = (bf16[128]{0:T(256)(128)(2,1)S(1)}, bf16[128]{0:T(256)(128)(2,1)}, u32[]{:S(2)}) copy-start(bf16[128]{0:T(256)(128)(2,1)} %param.29) | copy-start | bytes 772
  243.8 47.4 %copy-start.38 = (bf16[128]{0:T(256)(128)(2,1)S(1)}, bf16[128]{0:T(256)(128)(2,1)}, u32[]{:S(2)}) copy-start(bf16[128]{0:T(256)(128)(2,1)} %param.30) | copy-start | bytes 772
  243.8 65.5 %copy-start.35 = (bf16[512]{0:T(512)(128)(2,1)S(1)}, bf16[512]{0:T(512)(128)(2,1)}, u32[]{:S(2)}) copy-start(bf16[512]{0:T(512)(128)(2,1)} %param.32) | copy-start | bytes 3076
  243.8 91.9 %copy-start.39 = (bf16[128]{0:T(256)(128)(2,1)S(1)}, bf16[128]{0:T(256)(128)(2,1)}, u32[]{:S(2)}) copy-start(bf16[128]{0:T(256)(128)(2,1)} %param.34) | copy-start | bytes 772
  243.8 108.2 %copy-start.40 = (bf16[128]{0:T(256)(128)(2,1)S(1)}, bf16[128]{0:T(256)(128)(2,1)}, u32[]{:S(2)}) copy-start(bf16[128]{0:T(256)(128)(2,1)} %param.35) | copy-start | bytes 772
  243.9 126.7 %copy-start.41 = (bf16[128]{0:T(256)(128)(2,1)S(1)}, bf16[128]{0:T(256)(128)(2,1)}, u32[]{:S(2)}) copy-start(bf16[128]{0:T(256)(128)(2,1)} %param.36) | copy-start | bytes 772
  252.2 134.6 %all-to-all-start.1 = ((bf16[4,384,256]{1,2,0:T(8,128)(2,1)}), bf16[4,384,256]{1,2,0:T(8,128)(2,1)}, u32[]{:S(2)}, u32[]{:S(2)}) async-start(bf16[4,384,256]{1,2,0:T(8,128)(2,1)} %copy.70), calls=%async_computation.1 | async-start | bytes 1572864 | tf_op jit(solution)/shard_map/all_to_all | solution.py:114
  291.3 203.3 %copy-start.19 = (f32[8,1,128]{2,1,0:T(1,128)}, f32[8,1,128]{2,1,0:T(1,128)S(1)}, u32[]{:S(2)}) copy-start(f32[8,1,128]{2,1,0:T(1,128)S(1)} %convert_element_type.164) | copy-start | bytes 12292
  309.4 180.6 %copy-start.21 = (f32[8,1,128]{2,1,0:T(1,128)}, f32[8,1,128]{2,1,0:T(1,128)S(1)}, u32[]{:S(2)}) copy-start(f32[8,1,128]{2,1,0:T(1,128)S(1)} %convert_element_type.165) | copy-start | bytes 12292
  390.8 103.8 %copy-start.23 = (f32[384]{0:T(512)}, f32[384]{0:T(512)S(1)}, u32[]{:S(2)}) copy-start(f32[384]{0:T(512)S(1)} %broadcast_multiply_fusion.1) | copy-start | bytes 4612
  392.2 102.4 %copy-start.25 = (f32[384]{0:T(512)}, f32[384]{0:T(512)S(1)}, u32[]{:S(2)}) copy-start(f32[384]{0:T(512)S(1)} %fusion.66) | copy-start | bytes 4612
  463.0 9.3 copy-start.9
  474.6 15.4 slice-start
  476.0 14.0 copy-start.12
  476.0 14.0 copy-start.8
  476.0 14.0 slice-start.1
  490.0 4.6 copy-start.13
  494.6 3.4 copy-start.43
  495.1 1.2 copy-start.5
  495.2 4.7 copy-start.27
  502.2 15.9 all-to-all-start.2
  506.4 204.5 %reduce-scatter.13.cloned.1.call-start = ((), (), s32[]{:S(2)}) async-start(), calls=%async_computation.19 | async-start | bytes 4718592 | tf_op jit(solution)/shard_map/reduce_scatter | solution.py:222
  511.2 245.4 %reduce-scatter.11.cloned.1.call-start = ((), (), s32[]{:S(2)}) async-start(), calls=%async_computation.18 | async-start | bytes 4718592 | tf_op jit(solution)/shard_map/reduce_scatter | solution.py:221
  527.8 1.8 copy-start.3
  529.7 4.9 copy-start
  539.2 11.7 copy-start.1
  550.9 4.6 copy-start.4
  555.5 1.8 copy-start.3
  557.4 4.9 copy-start
  566.9 12.0 copy-start.1
  578.9 5.2 copy-start.4
  584.1 1.8 copy-start.3
  585.9 4.9 copy-start
  595.5 12.0 copy-start.1
  607.4 5.2 copy-start.4
  612.6 3.0 copy-start.2
  670.5 178.0 %reduce-scatter.7.cloned.1.call-start = ((), (), s32[]{:S(2)}) async-start(), calls=%async_computation.16 | async-start | bytes 4718592 | tf_op jit(solution)/shard_map/reduce_scatter | solution.py:219
  677.4 263.2 %reduce-scatter.9.cloned.1.call-start = ((), (), s32[]{:S(2)}) async-start(), calls=%async_computation.17 | async-start | bytes 4718592 | tf_op jit(solution)/shard_map/reduce_scatter | solution.py:220
  684.4 542.6 %reduce-scatter.15.cloned.1.call-start = ((), (), s32[]{:S(2)}) async-start(), calls=%async_computation.20 | async-start | bytes 18874368 | tf_op jit(solution)/shard_map/reduce_scatter | solution.py:154
  698.1 814.8 %reduce-scatter.17.cloned.1.call-start = ((), (), s32[]{:S(2)}) async-start(), calls=%async_computation.21 | async-start | bytes 18874368 | tf_op jit(solution)/shard_map/reduce_scatter | solution.py:155
  710.9 926.0 %all-reduce.14.cloned.1.call-start = ((), (), s32[]{:S(2)}) async-start(), calls=%async_computation.22 | async-start | bytes 12582912 | tf_op jit(solution)/shard_map/psum | solution.py:229
  1512.9 47.7 %copy-start.29 = (f32[1024]{0:T(1024)S(1)}, f32[1024]{0:T(1024)}, u32[]{:S(2)}) copy-start(f32[1024]{0:T(1024)} %get-tuple-element.254) | copy-start | bytes 12292
  1512.9 47.8 %copy-start.30 = (f32[1024]{0:T(1024)S(1)}, f32[1024]{0:T(1024)}, u32[]{:S(2)}) copy-start(f32[1024]{0:T(1024)} %get-tuple-element.315) | copy-start | bytes 12292
  1512.9 47.8 %copy-start.31 = (f32[1024]{0:T(1024)S(1)}, f32[1024]{0:T(1024)}, u32[]{:S(2)}) copy-start(f32[1024]{0:T(1024)} %get-tuple-element.319) | copy-start | bytes 12292
  1512.9 47.8 %copy-start.32 = (f32[4096]{0:T(1024)S(1)}, f32[4096]{0:T(1024)}, u32[]{:S(2)}) copy-start(f32[4096]{0:T(1024)} %get-tuple-element.317) | copy-start | bytes 49156
  1512.9 47.8 %copy-start.33 = (f32[1024]{0:T(1024)S(1)}, f32[1024]{0:T(1024)}, u32[]{:S(2)}) copy-start(f32[1024]{0:T(1024)} %get-tuple-element.252) | copy-start | bytes 12292
  1512.9 47.8 %copy-start.34 = (f32[1024]{0:T(1024)S(1)}, f32[1024]{0:T(1024)}, u32[]{:S(2)}) copy-start(f32[1024]{0:T(1024)} %get-tuple-element.260) | copy-start | bytes 12292
  1605.7 3.0 copy-start.11
  1605.7 3.0 copy-start.42
  1608.7 1.4 copy-start.6
  1608.7 2.1 copy-start.15
  1608.7 2.1 copy-start.28
  1636.9 6.3 copy-start.18
  1641.0 6.1 copy-start.16
  (7 other events, 5.4 us)
Sparse Core Ops, SparseCore 0:
  10.1 51.9 all-gather.17
  64.3 47.7 all-gather.15
  114.3 47.7 all-gather.19
  164.0 47.7 all-gather.21
  213.8 123.6 all-gather.23
  339.5 123.4 all-gather.25
  511.3 86.5 reduce-scatter.12
  670.6 85.9 reduce-scatter.10
  760.2 88.2 reduce-scatter.6
  852.4 88.2 reduce-scatter.8
  944.4 282.4 reduce-scatter.14
  1231.1 281.7 reduce-scatter.16
  1515.7 121.1 all-reduce.13
where the time goes:
time: 1660 us
  waiting for transfers between devices  1030 us (62%)
  blocking collectives  293 us (18%)
  matrix products  203 us (12%)
  local copies, waits for them, and re-layouts  70.2 us (4%)
  other arithmetic  31.7 us (2%)
    reduce_scatter x1, waiting for transfers between devices, local(): lax.psum_scatter(grad_in, 'fsdp', scatter_dimension=0, tiled=True)  286 us
    reduce_scatter x1, waiting for transfers between devices, local(): lax.psum_scatter(grad_out, 'fsdp', scatter_dimension=0, tiled=True)  286 us
    reduce_scatter x1, waiting for transfers between devices, local(): lax.psum_scatter(grad_key, 'fsdp', scatter_dimension=0, tiled=True)  92.2 us
    reduce_scatter x1, waiting for transfers between devices, local(): lax.psum_scatter(grad_query, 'fsdp', scatter_dimension=0, tiled=True)  91.9 us
    all_gather x1, waiting for transfers between devices, local(): lax.all_gather(out_weight, 'fsdp', axis=0, tiled=True)  49.8 us
    all_gather x1, waiting for transfers between devices, local(): lax.all_gather(query_weight, 'fsdp', axis=0, tiled=True)  47.1 us
    all_gather x1, waiting for transfers between devices, local(): lax.all_gather(value_weight, 'fsdp', axis=0, tiled=True)  46.5 us
    reduce_scatter x1, waiting for transfers between devices, local(): lax.psum_scatter(grad_value, 'fsdp', scatter_dimension=0, tiled=True)  45.6 us
  transfers between devices with their start and end apart: 16, of which 12 were waited for; matrix products, arithmetic and copies ran while one was open for 15% of the time, Pallas kernels for 0%

commit v1 on v0

--- a/solution.py
+++ b/solution.py
@@ -4,6 +4,10 @@
 from jax.sharding import PartitionSpec as P
 
 HD = 64
+
+
+def _resolve_shifts_all(xs, group_axis, dev_axis):
+    return lax.psum(lax.psum(xs, group_axis), dev_axis)
 
 
 def layer_norm(stream, gain, shift):
@@ -137,7 +141,7 @@
             jnp.sum(layer_out * layer_out),
         ]
     )
-    square_sums = lax.psum(squares, ("seq", "fsdp"))
+    square_sums = _resolve_shifts_all(squares, "fsdp", "seq")
     rms_values = jnp.sqrt(square_sums / single(token_rows * model_width * seq_count * fsdp_count))
     cotangent = out_cotangent.reshape(token_rows, model_width).astype(single)
     grad_stream, grad_gain_two, grad_shift_two = pull_second(cotangent)

time: 1660 us -> 1660 us (level)
  blocking collectives: 293 us -> 252 us
  waiting for transfers between devices: 1030 us -> 1070 us
    psum x1 -> x0, blocking collectives: 39.8 us -> none  [local(): square_sums = lax.psum(squares, ('seq', 'fsdp'))]
    psum x1, waiting for transfers between devices: 23.7 us -> 63.3 us  [local(): lax.psum((attn_summed[0], attn_summed[1], attn_summed[2], attn_summed[3],...]
where the time goes in v1:
time: 1660 us; the launch traced here: 1650 us
  waiting for transfers between devices  1070 us (64%)
  blocking collectives  252 us (15%)
  matrix products  203 us (12%)
  local copies, waits for them, and re-layouts  70.3 us (4%)
  other arithmetic  31.8 us (2%)
    reduce_scatter x1, waiting for transfers between devices, local(): lax.psum_scatter(grad_in, 'fsdp', scatter_dimension=0, tiled=True)  286 us
    reduce_scatter x1, waiting for transfers between devices, local(): lax.psum_scatter(grad_out, 'fsdp', scatter_dimension=0, tiled=True)  286 us
    reduce_scatter x1, waiting for transfers between devices, local(): lax.psum_scatter(grad_key, 'fsdp', scatter_dimension=0, tiled=True)  92.2 us
    reduce_scatter x1, waiting for transfers between devices, local(): lax.psum_scatter(grad_query, 'fsdp', scatter_dimension=0, tiled=True)  91.9 us
    psum x1, waiting for transfers between devices, local(): lax.psum((attn_summed[0], attn_summed[1], attn_summed[2], attn_summed[3],...  63.3 us
    all_gather x1, waiting for transfers between devices, local(): lax.all_gather(out_weight, 'fsdp', axis=0, tiled=True)  49.8 us
    all_gather x1, waiting for transfers between devices, local(): lax.all_gather(query_weight, 'fsdp', axis=0, tiled=True)  47.1 us
    all_gather x1, waiting for transfers between devices, local(): lax.all_gather(value_weight, 'fsdp', axis=0, tiled=True)  46.5 us
  transfers between devices with their start and end apart: 16, of which 12 were waited for; matrix products, arithmetic and copies ran while one was open for 15% of the time, Pallas kernels for 0%

profile of v1, /device:TPU:0, one launch (start us, length us, event | category | flops | bytes accessed | tf_op | source)
XLA Modules:
  0.0 1653.7 jit_solution(118266698120691608)
XLA Ops:
  10.6 22.4 %all-gather = bf16[8,1,128]{2,1,0:T(2,128)(2,1)S(1)} all-gather(bf16[1,1,128]{2,1,0:T(2,128)(2,1)} %bitcast.251), channel_id=1, replica_groups=mesh['seq'=4,'fsdp'=8] {'fsdp'}, dimensions={0}, use_global_device_ids=true | all-gather | bytes 2304 | tf_op jit(solution)/shard_map/all_gather | solution.py:65
  32.9 16.5 all-gather.1
  49.5 12.7 all-gather.18.cloned.1.call-done
  65.0 47.1 %all-gather.16.cloned.1.call-done = bf16[1024,1024]{1,0:T(8,128)(2,1)} async-done(((bf16[128,1024]{1,0:T(8,128)(2,1)}), bf16[1024,1024]{1,0:T(8,128)(2,1)}) %all-gather.16.cloned.1.call-update) | async-done | bytes 2097168 | tf_op jit(solution)/shard_map/all_gather | solution.py:61
  112.1 3.5 fusion.54
  115.6 46.5 %all-gather.20.cloned.1.call-done = bf16[1024,1024]{1,0:T(8,128)(2,1)} async-done(((bf16[128,1024]{1,0:T(8,128)(2,1)}), bf16[1024,1024]{1,0:T(8,128)(2,1)}) %all-gather.20.cloned.1.call-update) | async-done | bytes 2097168 | tf_op jit(solution)/shard_map/all_gather | solution.py:63
  165.0 3.8 copy.66
  168.8 3.8 all-to-all-start
  173.1 36.3 %all-to-all-done = bf16[3,384,1024]{1,0,2:T(4,128)(2,1)S(1)} async-done(((bf16[3,384,1024]{1,0,2:T(4,128)(2,1)}), bf16[3,384,1024]{1,0,2:T(4,128)(2,1)S(1)}, u32[]{:S(2)}, u32[]{:S(2)}) %all-to-all-start) | async-done | bytes 2359328 | tf_op jit(solution)/shard_map/all_to_all | solution.py:91
  218.6 25.2 %while.27 = (s32[]{:T(128)}, bf16[3,512,4,64]{1,3,2,0:T(8,128)(2,1)}, f32[3,4,512]{2,1,0:T(4,128)S(1)}, bf16[3,512,4,64]{1,3,2,0:T(8,128)(2,1)S(1)}, bf16[1536,4...) while((s32[]{:T(128)}, bf16[3,512,4,64]{1,3,2,0:T(8,128)(2,1)}, ...), condition=%wide.region_3.4_spmd, body=%wide.region_0.3_spmd.sunk | while | flops 833746944 | bytes 39912020 | solution.py:116
  222.8 4.2 fusion.137
  231.2 4.2 fusion.137
  239.6 4.2 fusion.137
  246.7 3.4 all_to_all.51
  252.2 4.2 all-to-all-start.1
  256.5 18.1 %all-gather.2 = bf16[8,1,128]{2,1,0:T(2,128)(2,1)S(1)} all-gather(bf16[1,1,128]{2,1,0:T(2,128)(2,1)S(1)} %bitcast.253), channel_id=1, replica_groups=mesh['seq'=4,'fsdp'=8] {'fsdp'}, dimensions={0}, use_global_device_ids=true | all-gather | bytes 2304 | tf_op jit(solution)/shard_map/all_gather | solution.py:67
  274.5 16.7 %all-gather.3 = bf16[8,1,128]{2,1,0:T(2,128)(2,1)S(1)} all-gather(bf16[1,1,128]{2,1,0:T(2,128)(2,1)S(1)} %bitcast.254), channel_id=1, replica_groups=mesh['seq'=4,'fsdp'=8] {'fsdp'}, dimensions={0}, use_global_device_ids=true | all-gather | bytes 2304 | tf_op jit(solution)/shard_map/all_gather | solution.py:68
  291.3 18.1 %all-gather.4 = bf16[8,1,128]{2,1,0:T(2,128)(2,1)S(1)} all-gather(bf16[1,1,128]{2,1,0:T(2,128)(2,1)S(1)} %bitcast.255), channel_id=1, replica_groups=mesh['seq'=4,'fsdp'=8] {'fsdp'}, dimensions={0}, use_global_device_ids=true | all-gather | bytes 2304 | tf_op jit(solution)/shard_map/all_gather | solution.py:69
  309.4 26.3 %all-gather.5 = bf16[8,1,512]{2,1,0:T(2,128)(2,1)S(1)} all-gather(bf16[1,1,512]{2,1,0:T(2,128)(2,1)S(1)} %reshape.201), channel_id=1, replica_groups=mesh['seq'=4,'fsdp'=8] {'fsdp'}, dimensions={0}, use_global_device_ids=true | all-gather | bytes 9216 | tf_op jit(solution)/shard_map/all_gather | solution.py:74
  335.7 16.3 all-gather.6
  352.0 18.5 %all-gather.7 = bf16[8,1,128]{2,1,0:T(2,128)(2,1)S(1)} all-gather(bf16[1,1,128]{2,1,0:T(2,128)(2,1)S(1)} %bitcast.257), channel_id=1, replica_groups=mesh['seq'=4,'fsdp'=8] {'fsdp'}, dimensions={0}, use_global_device_ids=true | all-gather | bytes 2304 | tf_op jit(solution)/shard_map/all_gather | solution.py:76
  370.5 16.3 all-gather.8
  386.9 3.9 fusion.75
  392.2 20.9 %multiply_convert_fusion.1 = (bf16[384,4096]{1,0:T(8,128)(2,1)}, f32[384,4096]{1,0:T(8,128)}, f32[384,4096]{1,0:T(8,128)}) fusion(f32[4096]{0:T(1024)S(1)} %bitcast.246, bf16[1024,4096]{1,0:T(8,128)(2,1)} %all-gather.24.cloned.1.call-done, f32[384,1024]{1,0:T(8,128)} %copy-done.7, f32[1024]{0:T(1024)S(1)} %bitcast.235, f32[1024]{0:T(1024)S(1)} %bitcast.230, ...), kind=kOutput, calls=%fused_computation.50 | convolution fusion | flops 3327000576 | bytes 25717760 | tf_op jit(solution)/shard_map/dot_general | solution.py:126
  413.2 49.8 %all-gather.26.cloned.1.call-done = bf16[4096,1024]{1,0:T(8,128)(2,1)} async-done(((bf16[512,1024]{1,0:T(8,128)(2,1)}), bf16[4096,1024]{1,0:T(8,128)(2,1)}) %all-gather.26.cloned.1.call-update) | async-done | bytes 8388624 | tf_op jit(solution)/shard_map/all_gather | solution.py:73
  463.0 9.0 fusion.73
  476.0 14.0 convert_reduce_fusion
  490.0 4.5 multiply_reduce_fusion.6
  502.2 4.2 all-to-all-start.2
  506.5 4.7 fusion.80
  511.2 6.9 all-to-all-done.2
  520.8 3.8 reshape.189
  527.9 84.8 %while.28 = (s32[]{:T(128)}, f32[1536,4,64]{0,2,1:T(8,128)}, f32[1536,4,64]{0,2,1:T(8,128)}, bf16[3,512,4,64]{1,3,2,0:T(8,128)(2,1)}, bf16[3,512,4,64]{1,3,2,0:T...) while((s32[]{:T(128)}, f32[1536,4,64]{0,2,1:T(8,128)}, ...), condition=%wide.region_14.15_spmd.clone, body=%wide.region_12.14_spmd.clone.sunk | while | flops 2053240832 | bytes 211347216 | solution.py:200
  529.8 4.9 multiply_reduce_fusion.13
  534.7 4.6 multiply_convert_fusion.3
  539.3 5.3 fusion.148
  544.6 6.4 fusion.150
  550.9 4.6 fusion.149
  557.5 4.9 multiply_reduce_fusion.13
  562.3 4.6 multiply_convert_fusion.3
  566.9 5.8 fusion.148
  572.7 6.3 fusion.150
  579.0 5.2 fusion.149
  586.0 4.9 multiply_reduce_fusion.13
  590.9 4.6 multiply_convert_fusion.3
  595.5 5.8 fusion.148
  601.3 6.2 fusion.150
  607.5 5.2 fusion.149
  619.0 4.3 copy.76
  623.3 39.6 %all_to_all.65 = bf16[3,1536,256]{2,0,1:T(4,128)(2,1)S(1)} all-to-all(bf16[3,1536,256]{2,0,1:T(4,128)(2,1)S(1)} %copy.76), channel_id=1, replica_groups=mesh['seq'=4,'fsdp'=8] {'seq'}, dimensions={1} | all-to-all | bytes 4718592 | tf_op jit(solution)/shard_map/all_to_all | solution.py:210
  666.2 4.3 convolution_bitcast_fusion
  672.9 4.6 convolution_bitcast_fusion.2
  679.8 4.5 convolution_bitcast_fusion.1
  685.1 13.1 fusion.68
  698.5 12.5 fusion.81
  711.0 45.6 %reduce-scatter.11.cloned.1.call-done = f32[128,1024]{0,1:T(8,128)} async-done(((f32[1024,1024]{0,1:T(8,128)}), f32[128,1024]{0,1:T(8,128)}) %reduce-scatter.11.cloned.1.call-update) | async-done | bytes 524304 | tf_op jit(solution)/shard_map/reduce_scatter | solution.py:225
  756.6 91.9 %reduce-scatter.7.cloned.1.call-done = f32[128,1024]{0,1:T(8,128)} async-done(((f32[1024,1024]{0,1:T(8,128)}), f32[128,1024]{0,1:T(8,128)}) %reduce-scatter.7.cloned.1.call-update) | async-done | bytes 524304 | tf_op jit(solution)/shard_map/reduce_scatter | solution.py:223
  848.5 92.2 %reduce-scatter.9.cloned.1.call-done = f32[128,1024]{0,1:T(8,128)} async-done(((f32[1024,1024]{0,1:T(8,128)}), f32[128,1024]{0,1:T(8,128)}) %reduce-scatter.9.cloned.1.call-update) | async-done | bytes 524304 | tf_op jit(solution)/shard_map/reduce_scatter | solution.py:224
  940.7 286.2 %reduce-scatter.15.cloned.1.call-done = f32[128,4096]{1,0:T(8,128)} async-done(((f32[1024,4096]{1,0:T(8,128)}), f32[128,4096]{1,0:T(8,128)}) %reduce-scatter.15.cloned.1.call-update) | async-done | bytes 2097168 | tf_op jit(solution)/shard_map/reduce_scatter | solution.py:158
  1226.9 285.9 %reduce-scatter.17.cloned.1.call-done = f32[512,1024]{1,0:T(8,128)} async-done(((f32[4096,1024]{1,0:T(8,128)}), f32[512,1024]{1,0:T(8,128)}) %reduce-scatter.17.cloned.1.call-update) | async-done | bytes 2097168 | tf_op jit(solution)/shard_map/reduce_scatter | solution.py:159
  1516.6 3.3 stack.45
  1520.2 35.7 %all-reduce.9 = (f32[1024]{0:T(1024)S(1)}, f32[1024]{0:T(1024)S(1)}, f32[1024]{0:T(1024)S(1)}, f32[1024]{0:T(1024)S(1)}, f32[1024]{0:T(1024)S(1)}, /*index=5*/f3...) all-reduce(f32[1024]{0:T(1024)S(1)} %bitcast.244, ...), channel_id=6, replica_groups=mesh['seq'=4,'fsdp'=8] {'fsdp'}, use_global_device_ids=true, to_apply=%region_24.25.clone | all-reduce | flops 12293 | bytes 98344
  1556.6 7.4 all-reduce.10
  1572.1 63.3 %all-reduce.14.cloned.1.call-done = (f32[128,1024]{0,1:T(8,128)}, f32[128,1024]{0,1:T(8,128)}, f32[128,1024]{0,1:T(8,128)}, f32[128,1024]{1,0:T(8,128)}, f32[128,4096]{1,0:T(8,128)}, /*index=5*/f32[512,1024]{1,0:T(8,128)}) async-done(((f32[128,1024]{0,1:T(8,128)}, f32[128,1024]{0,1:T(8,128)}, f32[128,1024]{0,1:T(8,128)}, f32[128,1024]{1,0:T(8,128)}, f32[128,4096]{1,0:T(8,128)}, ...) | async-done | bytes 6291472 | tf_op jit(solution)/shard_map/psum | solution.py:233
  (235 shorter events, 99.3 us)
Async XLA Ops:
  7.2 55.0 %all-gather.18.cloned.1.call-start = ((), (), s32[]{:S(2)}) async-start(), calls=%async_computation.11 | async-start | bytes 2359296 | tf_op jit(solution)/shard_map/all_gather | solution.py:62
  7.9 104.2 %all-gather.16.cloned.1.call-start = ((), (), s32[]{:S(2)}) async-start(), calls=%async_computation.10 | async-start | bytes 2359296 | tf_op jit(solution)/shard_map/all_gather | solution.py:61
  8.7 153.4 %all-gather.20.cloned.1.call-start = ((), (), s32[]{:S(2)}) async-start(), calls=%async_computation.12 | async-start | bytes 2359296 | tf_op jit(solution)/shard_map/all_gather | solution.py:63
  9.4 377.5 %all-gather.22.cloned.1.call-start = ((), (), s32[]{:S(2)}) async-start(), calls=%async_computation.13 | async-start | bytes 2359296 | tf_op jit(solution)/shard_map/all_gather | solution.py:64
  10.0 102.1 %copy-start.10 = (bf16[1,384,1024]{2,1,0:T(8,128)(2,1)S(1)}, bf16[1,384,1024]{2,1,0:T(8,128)(2,1)}, u32[]{:S(2)}) copy-start(bf16[1,384,1024]{2,1,0:T(8,128)(2,1)} %param.21) | copy-start | bytes 2359300
  10.0 382.2 %all-gather.24.cloned.1.call-start = ((), (), s32[]{:S(2)}) async-start(), calls=%async_computation.14 | async-start | bytes 9437184 | tf_op jit(solution)/shard_map/all_gather | solution.py:72
  162.1 2.7 copy-start.17
  168.8 40.7 %all-to-all-start = ((bf16[3,384,1024]{1,0,2:T(4,128)(2,1)}), bf16[3,384,1024]{1,0,2:T(4,128)(2,1)S(1)}, u32[]{:S(2)}, u32[]{:S(2)}) async-start(bf16[3,384,1024]{1,0,2:T(4,128)(2,1)} %copy.66), calls=%async_computation | async-start | bytes 6291456 | tf_op jit(solution)/shard_map/all_to_all | solution.py:91
  172.5 290.4 %all-gather.26.cloned.1.call-start = ((), (), s32[]{:S(2)}) async-start(), calls=%async_computation.15 | async-start | bytes 9437184 | tf_op jit(solution)/shard_map/all_gather | solution.py:73
  243.8 12.6 copy-start.36
  243.8 30.7 %copy-start.37 = (bf16[128]{0:T(256)(128)(2,1)S(1)}, bf16[128]{0:T(256)(128)(2,1)}, u32[]{:S(2)}) copy-start(bf16[128]{0:T(256)(128)(2,1)} %param.29) | copy-start | bytes 772
  243.8 47.4 %copy-start.38 = (bf16[128]{0:T(256)(128)(2,1)S(1)}, bf16[128]{0:T(256)(128)(2,1)}, u32[]{:S(2)}) copy-start(bf16[128]{0:T(256)(128)(2,1)} %param.30) | copy-start | bytes 772
  243.8 65.5 %copy-start.35 = (bf16[512]{0:T(512)(128)(2,1)S(1)}, bf16[512]{0:T(512)(128)(2,1)}, u32[]{:S(2)}) copy-start(bf16[512]{0:T(512)(128)(2,1)} %param.32) | copy-start | bytes 3076
  243.8 91.9 %copy-start.39 = (bf16[128]{0:T(256)(128)(2,1)S(1)}, bf16[128]{0:T(256)(128)(2,1)}, u32[]{:S(2)}) copy-start(bf16[128]{0:T(256)(128)(2,1)} %param.34) | copy-start | bytes 772
  243.8 108.1 %copy-start.40 = (bf16[128]{0:T(256)(128)(2,1)S(1)}, bf16[128]{0:T(256)(128)(2,1)}, u32[]{:S(2)}) copy-start(bf16[128]{0:T(256)(128)(2,1)} %param.35) | copy-start | bytes 772
  243.9 126.7 %copy-start.41 = (bf16[128]{0:T(256)(128)(2,1)S(1)}, bf16[128]{0:T(256)(128)(2,1)}, u32[]{:S(2)}) copy-start(bf16[128]{0:T(256)(128)(2,1)} %param.36) | copy-start | bytes 772
  252.2 134.6 %all-to-all-start.1 = ((bf16[4,384,256]{1,2,0:T(8,128)(2,1)}), bf16[4,384,256]{1,2,0:T(8,128)(2,1)}, u32[]{:S(2)}, u32[]{:S(2)}) async-start(bf16[4,384,256]{1,2,0:T(8,128)(2,1)} %copy.70), calls=%async_computation.1 | async-start | bytes 1572864 | tf_op jit(solution)/shard_map/all_to_all | solution.py:118
  291.3 203.3 %copy-start.19 = (f32[8,1,128]{2,1,0:T(1,128)}, f32[8,1,128]{2,1,0:T(1,128)S(1)}, u32[]{:S(2)}) copy-start(f32[8,1,128]{2,1,0:T(1,128)S(1)} %convert_element_type.164) | copy-start | bytes 12292
  309.4 180.6 %copy-start.21 = (f32[8,1,128]{2,1,0:T(1,128)}, f32[8,1,128]{2,1,0:T(1,128)S(1)}, u32[]{:S(2)}) copy-start(f32[8,1,128]{2,1,0:T(1,128)S(1)} %convert_element_type.165) | copy-start | bytes 12292
  390.8 103.8 %copy-start.23 = (f32[384]{0:T(512)}, f32[384]{0:T(512)S(1)}, u32[]{:S(2)}) copy-start(f32[384]{0:T(512)S(1)} %broadcast_multiply_fusion.1) | copy-start | bytes 4612
  392.2 102.4 %copy-start.25 = (f32[384]{0:T(512)}, f32[384]{0:T(512)S(1)}, u32[]{:S(2)}) copy-start(f32[384]{0:T(512)S(1)} %fusion.66) | copy-start | bytes 4612
  463.0 9.3 copy-start.9
  474.6 15.4 slice-start
  476.0 14.0 copy-start.12
  476.0 14.0 copy-start.8
  476.0 14.0 slice-start.1
  490.0 4.6 copy-start.13
  494.6 3.4 copy-start.43
  495.1 1.2 copy-start.5
  495.2 4.7 copy-start.27
  502.2 15.9 all-to-all-start.2
  506.4 204.6 %reduce-scatter.13.cloned.1.call-start = ((), (), s32[]{:S(2)}) async-start(), calls=%async_computation.19 | async-start | bytes 4718592 | tf_op jit(solution)/shard_map/reduce_scatter | solution.py:226
  511.2 245.4 %reduce-scatter.11.cloned.1.call-start = ((), (), s32[]{:S(2)}) async-start(), calls=%async_computation.18 | async-start | bytes 4718592 | tf_op jit(solution)/shard_map/reduce_scatter | solution.py:225
  527.9 1.8 copy-start.3
  529.7 4.9 copy-start
  539.3 11.7 copy-start.1
  550.9 4.6 copy-start.4
  555.6 1.8 copy-start.3
  557.4 4.9 copy-start
  566.9 12.0 copy-start.1
  579.0 5.2 copy-start.4
  584.1 1.8 copy-start.3
  586.0 4.9 copy-start
  595.5 12.0 copy-start.1
  607.5 5.2 copy-start.4
  612.7 3.0 copy-start.2
  670.5 178.0 %reduce-scatter.7.cloned.1.call-start = ((), (), s32[]{:S(2)}) async-start(), calls=%async_computation.16 | async-start | bytes 4718592 | tf_op jit(solution)/shard_map/reduce_scatter | solution.py:223
  677.5 263.2 %reduce-scatter.9.cloned.1.call-start = ((), (), s32[]{:S(2)}) async-start(), calls=%async_computation.17 | async-start | bytes 4718592 | tf_op jit(solution)/shard_map/reduce_scatter | solution.py:224
  684.4 542.4 %reduce-scatter.15.cloned.1.call-start = ((), (), s32[]{:S(2)}) async-start(), calls=%async_computation.20 | async-start | bytes 18874368 | tf_op jit(solution)/shard_map/reduce_scatter | solution.py:158
  698.2 814.6 %reduce-scatter.17.cloned.1.call-start = ((), (), s32[]{:S(2)}) async-start(), calls=%async_computation.21 | async-start | bytes 18874368 | tf_op jit(solution)/shard_map/reduce_scatter | solution.py:159
  710.9 924.5 %all-reduce.14.cloned.1.call-start = ((), (), s32[]{:S(2)}) async-start(), calls=%async_computation.22 | async-start | bytes 12582912 | tf_op jit(solution)/shard_map/psum | solution.py:233
  1512.8 7.4 copy-start.29
  1512.8 7.4 copy-start.30
  1512.8 7.4 copy-start.31
  1512.8 7.4 copy-start.32
  1512.8 7.4 copy-start.33
  1512.8 7.4 copy-start.34
  1564.5 3.0 copy-start.11
  1564.5 3.0 copy-start.42
  1567.6 1.4 copy-start.6
  1567.6 2.1 copy-start.15
  1567.6 2.1 copy-start.28
  1635.4 6.3 copy-start.18
  1639.5 6.1 copy-start.16
  (7 other events, 5.4 us)
Sparse Core Ops, SparseCore 0:
  10.1 51.9 all-gather.17
  64.3 47.7 all-gather.15
  114.3 47.7 all-gather.19
  164.0 47.7 all-gather.21
  213.8 123.6 all-gather.23
  339.5 123.4 all-gather.25
  511.3 86.6 reduce-scatter.12
  670.7 85.9 reduce-scatter.10
  760.3 88.2 reduce-scatter.6
  852.4 88.1 reduce-scatter.8
  944.5 282.3 reduce-scatter.14
  1231.0 281.7 reduce-scatter.16
  1515.5 119.8 all-reduce.13
